TPU v7x, 128 devices: a whole 4x4x4 slice. The times are simulated.
128 devices in a mesh: req: 16 (over y, z), mlp: 8 (over x, core).
Axes of the slice: x: 4, y: 4, z: 4, core: 2. Of those that a mesh axis runs over, the one named last changes fastest.
Arguments:
- blocks: bfloat16 [2048, 4096], P('req'), may hold values from -6 to 6
- token_embed: bfloat16 [2048, 4096], P('req'), may hold values from -6 to 6
- accepted: int32 [2048], P('req'), may hold values 0 or 1
- prompt_len: int32 [16], P('req'), may hold values from 2 to 512, as said below
- cache_len: int32 [16, 8], P('req'), may hold values from 1 to 1024, as said below
- prompt_kv: bfloat16 [16, 512, 2048], P('req', None, 'mlp'), may hold values from -364 to 364
- cache_kv: bfloat16 [16, 8, 1024, 2048], P('req', None, None, 'mlp'), may hold values from -6 to 6
- attn_gain: float32 [4096], replicated, may hold values from 0.25 to 1.75
- w_q: bfloat16 [4096, 4096], P(None, 'mlp'), may hold values from -0.09375 to 0.09375
- w_kv: bfloat16 [4096, 2048], P(None, 'mlp'), may hold values from -0.09375 to 0.09375
- w_o: bfloat16 [4096, 4096], P('mlp'), may hold values from -0.09375 to 0.09375
- mlp_gain: float32 [4096], replicated, may hold values from 0.25 to 1.75
- w_gate: bfloat16 [4096, 7168], P('req', 'mlp'), may hold values from -0.09375 to 0.09375
- w_up: bfloat16 [4096, 7168], P('req', 'mlp'), may hold values from -0.09375 to 0.09375
- w_down: bfloat16 [7168, 4096], P('mlp'), may hold values from -0.0625 to 0.0625
Outputs:
- denoised: bfloat16 [2048, 4096], P('req')
Inputs may be any that keep to these rules, and one draw needn't show every extreme that they name: `prompt_len`: shared by the 8 requests of a group; some group has a prompt of exactly 512. `cache_len`: every group has a request with exactly 1024 cached tokens.
All inputs are finite; a program needn't handle non-finite values. No bound on the sum of `accepted` on one device may be relied on, other than what follows from the above.
Results may differ from a plain program's by a relative error of at most 0.022.
Values may be sent and summed in bfloat16 or wider, within the bound.
A program may use at most 128 MiB of HBM per device.

v0:
```python
import math
import jax
import jax.numpy as jnp
from jax import lax
from jax.sharding import PartitionSpec as P

HEAD_DIM = 128
REQS = 8
BLOCK = 16
EPSILON = 1e-05
THETA = 500000.0


def rms_scale(stream, gain):
    widened = stream.astype(jnp.float32)
    mean_square = jnp.mean(widened * widened, axis=-1, keepdims=True)
    return (widened * lax.rsqrt(mean_square + EPSILON) * gain).astype(jnp.bfloat16)


def rope(values, positions):
    head_size = values.shape[-1]
    half_size = head_size // 2
    frequency = THETA ** (-2.0 * jnp.arange(half_size, dtype=jnp.float32) / head_size)
    angles = positions.astype(jnp.float32)[:, None] * frequency[None, :]
    cosine = jnp.cos(angles)[:, None, :]
    sine = jnp.sin(angles)[:, None, :]
    first = values[..., :half_size]
    second = values[..., half_size:]
    return jnp.concatenate(
        [first * cosine - second * sine, second * cosine + first * sine], axis=-1
    )


def attend_one(
    queries, block_keys, block_values, prompt_part, cached_part, prompt_size, cache_size
):
    block_len, head_count, head_size = queries.shape
    kv_heads = block_keys.shape[1]
    group_size = head_count // kv_heads
    grouped = queries.reshape(block_len, kv_heads, group_size, head_size)
    scale = 1.0 / math.sqrt(head_size)

    def scores(keys):
        return (
            jnp.einsum("tkgd,lkd->kgtl", grouped, keys, preferred_element_type=jnp.float32) * scale
        )

    prompt_score = scores(prompt_part[:, :, 0])
    cache_score = scores(cached_part[:, :, 0])
    block_score = scores(block_keys)
    prompt_ok = jnp.arange(prompt_part.shape[0], dtype=jnp.int32) < prompt_size
    cache_ok = jnp.arange(cached_part.shape[0], dtype=jnp.int32) < cache_size
    prompt_score = jnp.where(prompt_ok, prompt_score, -1e30)
    cache_score = jnp.where(cache_ok, cache_score, -1e30)
    largest = jnp.maximum(
        jnp.maximum(
            jnp.max(prompt_score, -1, keepdims=True), jnp.max(cache_score, -1, keepdims=True)
        ),
        jnp.max(block_score, -1, keepdims=True),
    )
    prompt_exp = jnp.exp(prompt_score - largest)
    cache_exp = jnp.exp(cache_score - largest)
    block_exp = jnp.exp(block_score - largest)
    total = (
        jnp.sum(prompt_exp, -1, keepdims=True)
        + jnp.sum(cache_exp, -1, keepdims=True)
        + jnp.sum(block_exp, -1, keepdims=True)
    )
    prompt_w = (prompt_exp / total).astype(jnp.bfloat16)
    cache_w = (cache_exp / total).astype(jnp.bfloat16)
    block_w = (block_exp / total).astype(jnp.bfloat16)
    result = jnp.einsum(
        "kgtl,lkd->tkgd", prompt_w, prompt_part[:, :, 1], preferred_element_type=jnp.float32
    )
    result = result + jnp.einsum(
        "kgtl,lkd->tkgd", cache_w, cached_part[:, :, 1], preferred_element_type=jnp.float32
    )
    result = result + jnp.einsum(
        "kgtl,lkd->tkgd", block_w, block_values, preferred_element_type=jnp.float32
    )
    return result.reshape(block_len, head_count * head_size).astype(jnp.bfloat16)


def swiglu(gate, up_part):
    return (jax.nn.silu(gate) * up_part).astype(jnp.bfloat16)


def body(
    blocks,
    token_embed,
    accepted,
    prompt_len,
    cache_len,
    prompt_kv,
    cache_kv,
    attn_gain,
    w_q,
    w_kv,
    w_o,
    mlp_gain,
    w_gate,
    w_up,
    w_down,
):
    row_count = blocks.shape[0]
    prompt_size = prompt_len[0]
    cache_sizes = cache_len[0]
    positions = (
        prompt_size + cache_sizes[:, None] + jnp.arange(BLOCK, dtype=jnp.int32)[None, :]
    ).reshape(-1)
    local_kv = w_kv.shape[1] // (2 * HEAD_DIM)
    local_heads = w_q.shape[1] // HEAD_DIM
    prompt_part = prompt_kv[0].reshape(-1, local_kv, 2, HEAD_DIM)
    cached = cache_kv[0].reshape(REQS, -1, local_kv, 2, HEAD_DIM)

    def one_pass(stream):
        normed = rms_scale(stream, attn_gain)
        queries = rope(
            jnp.dot(normed, w_q, preferred_element_type=jnp.float32).reshape(
                row_count, local_heads, HEAD_DIM
            ),
            positions,
        ).astype(jnp.bfloat16)
        key_value = jnp.dot(normed, w_kv, preferred_element_type=jnp.float32).reshape(
            row_count, local_kv, 2, HEAD_DIM
        )
        keys = rope(key_value[:, :, 0], positions).astype(jnp.bfloat16)
        values = key_value[:, :, 1].astype(jnp.bfloat16)

        def attend_request(items):
            query_part, key_part, value_part, cache_part, cache_size = items
            return attend_one(
                query_part, key_part, value_part, prompt_part, cache_part, prompt_size, cache_size
            )

        attended = lax.map(
            attend_request,
            (
                queries.reshape(REQS, BLOCK, local_heads, HEAD_DIM),
                keys.reshape(REQS, BLOCK, local_kv, HEAD_DIM),
                values.reshape(REQS, BLOCK, local_kv, HEAD_DIM),
                cached,
                cache_sizes,
            ),
        )
        attended = attended.reshape(row_count, local_heads * HEAD_DIM)
        mixed = lax.psum(jnp.dot(attended, w_o, preferred_element_type=jnp.float32), "mlp")
        after_attn = (stream.astype(jnp.float32) + mixed).astype(jnp.bfloat16)
        normed2 = rms_scale(after_attn, mlp_gain)
        pass_gate, pass_up = (
            lax.all_gather(w_gate, "req", axis=0, tiled=True),
            lax.all_gather(w_up, "req", axis=0, tiled=True),
        )
        gate = jnp.dot(normed2, pass_gate, preferred_element_type=jnp.float32)
        up_part = jnp.dot(normed2, pass_up, preferred_element_type=jnp.float32)
        hidden = swiglu(gate, up_part)
        down = lax.psum(jnp.dot(hidden, w_down, preferred_element_type=jnp.float32), "mlp")
        return (after_attn.astype(jnp.float32) + down).astype(jnp.bfloat16)

    first = one_pass(blocks)
    second_input = jnp.where(accepted[:, None] == 1, token_embed, first)
    return one_pass(second_input)


def solution(mesh):
    return jax.shard_map(
        body,
        mesh=mesh,
        in_specs=(
            P("req", None),
            P("req", None),
            P("req"),
            P("req"),
            P("req", None),
            P("req", None, "mlp"),
            P("req", None, None, "mlp"),
            P(),
            P(None, "mlp"),
            P(None, "mlp"),
            P("mlp", None),
            P(),
            P("req", "mlp"),
            P("req", "mlp"),
            P("mlp", None),
        ),
        out_specs=P("req", None),
        check_vma=False,
    )
```

profile of v0, /device:TPU:0, one launch (start us, length us, event | category | flops | bytes accessed | tf_op | source)
XLA Modules:
  0.0 504.8 jit_solution(11946350769607813790)
XLA Ops:
  7.4 1.7 fusion.76
  9.3 1.8 fusion.119
  11.2 0.7 slice.83
  12.8 2.9 fusion.121
  16.4 1.0 fusion.134
  17.3 1.4 copy.63
  18.8 6.4 %copy.26 = bf16[1,8,1024,256]{2,3,1,0:T(8,128)(2,1)} copy(bf16[1,8,1024,256]{3,2,1,0:T(8,128)(2,1)} %param.25) | data formatting | bytes 8388608 | tf_op args[6]
  25.2 6.5 %copy.30 = bf16[8,1024,1,2,128]{4,1,3,2,0:T(8,128)(2,1)} copy(bf16[8,1024,1,2,128]{1,4,3,0,2:T(8,128)(2,1)} %bitcast.294) | data formatting | bytes 8388608 | tf_op jit(solution)/shard_map/while | solution.py:136
  32.2 0.9 pad_maximum_fusion.2
  33.1 45.7 %while.20 = (s32[]{:T(128)}, bf16[8,16,512]{2,1,0:T(8,128)(2,1)S(1)}, s32[]{:T(128)}, bf16[8,16,4,128]{3,1,0,2:T(8,128)(2,1)S(1)}, bf16[512,1,2,128]{3,0,2,1:T(8...) while((s32[]{:T(128)}, ...), condition=%wide.region_8.9_spmd, body=%wide.region_1.8_spmd.sunk | while | flops 51675520 | bytes 3347849 | solution.py:136
  33.1 1.1 dynamic-slice_bitcast_fusion.4
  34.2 0.7 dynamic_slice.112
  34.9 0.7 iota_compare_fusion.8
  37.9 0.9 fusion.211
  38.8 1.1 dynamic-slice_bitcast_fusion.4
  39.9 0.7 dynamic_slice.112
  40.6 0.7 iota_compare_fusion.8
  43.6 0.9 fusion.211
  44.5 1.1 dynamic-slice_bitcast_fusion.4
  45.6 0.7 dynamic_slice.112
  46.3 0.7 iota_compare_fusion.8
  49.3 0.9 fusion.211
  50.2 1.1 dynamic-slice_bitcast_fusion.4
  52.0 0.7 iota_compare_fusion.8
  55.0 0.9 fusion.211
  56.0 1.1 dynamic-slice_bitcast_fusion.4
  57.7 0.7 iota_compare_fusion.8
  60.7 0.9 fusion.211
  61.7 1.1 dynamic-slice_bitcast_fusion.4
  63.4 0.7 iota_compare_fusion.8
  66.4 0.9 fusion.211
  67.4 1.1 dynamic-slice_bitcast_fusion.4
  69.1 0.7 iota_compare_fusion.8
  72.1 0.9 fusion.211
  73.1 1.1 dynamic-slice_bitcast_fusion.4
  74.8 0.7 iota_compare_fusion.8
  77.8 0.9 fusion.211
  78.8 4.2 fusion.154
  84.3 68.4 %all-reduce.5.cloned.1.call-done = f32[128,4096]{1,0:T(8,128)} async-done(((f32[128,4096]{1,0:T(8,128)}), f32[128,4096]{1,0:T(8,128)}) %all-reduce.5.cloned.1.call-update) | async-done | bytes 2097168 | tf_op jit(solution)/shard_map/psum | solution.py:147
  152.7 2.3 fusion.80
  155.5 5.2 %fusion.117 = f32[128,896]{1,0:T(8,128)} fusion(bf16[4096,896]{1,0:T(8,128)(2,1)} %all-gather.3.cloned.1.call-done, bf16[128,4096]{1,0:T(8,128)(2,1)S(1)} %get-tuple-element.160, f32[4096]{0:T(1024)S(1)} %copy-done.6, f32[128]{0:T(128)} %add_rsqrt_fusion.2), kind=kOutput, calls=%fused_computation.162 | convolution fusion | flops 941621248 | bytes 8864256 | tf_op jit(solution)/shard_map/dot_general | solution.py:154
  160.7 61.8 %all-gather.5.cloned.1.call-done = bf16[4096,896]{1,0:T(8,128)(2,1)} async-done(((bf16[256,896]{1,0:T(8,128)(2,1)}), bf16[4096,896]{1,0:T(8,128)(2,1)}) %all-gather.5.cloned.1.call-update) | async-done | bytes 7340048 | tf_op jit(solution)/shard_map/all_gather | solution.py:152
  222.5 9.0 %fusion.96 = f32[128,4096]{1,0:T(8,128)} fusion(bf16[896,4096]{1,0:T(8,128)(2,1)} %param.33, bf16[4096,896]{1,0:T(8,128)(2,1)} %all-gather.5.cloned.1.call-done, f32[128,896]{1,0:T(8,128)} %fusion.117, bf16[128,4096]{1,0:T(8,128)(2,1)S(1)} %get-tuple-element.160, f32[4096]{0:T(1024)S(1)} %copy-done.6, f32[128]{0:T(128)} %add_rsqrt_fusion.2), kind=kOutput, calls=%fused_computation.148 | convolution fusion | flops 1881833472 | bytes 18301440 | tf_op jit(solution)/shard_map/dot_general | solution.py:157
  231.8 1.2 broadcast_compare_fusion
  233.0 63.9 %all-reduce.7.cloned.1.call-done = f32[128,4096]{1,0:T(8,128)} async-done(((f32[128,4096]{1,0:T(8,128)}), f32[128,4096]{1,0:T(8,128)}) %all-reduce.7.cloned.1.call-update) | async-done | bytes 2097168 | tf_op jit(solution)/shard_map/psum | solution.py:157
  296.9 2.5 fusion.84
  299.4 1.0 copy-done.3
  301.1 3.3 fusion.113
  305.4 39.2 %while.21 = (s32[]{:T(128)}, bf16[8,16,512]{2,1,0:T(8,128)(2,1)S(1)}, s32[]{:T(128)}, bf16[8,16,4,128]{3,1,0,2:T(8,128)(2,1)S(1)}, bf16[512,1,2,128]{3,0,2,1:T(8...) while((s32[]{:T(128)}, ...), condition=%wide.region_20.21_spmd, body=%wide.region_13.20_spmd.sunk | while | flops 51675520 | bytes 3379597 | solution.py:136
  305.4 1.1 dynamic-slice_bitcast_fusion.5
  310.3 1.1 dynamic-slice_bitcast_fusion.5
  315.2 1.1 dynamic-slice_bitcast_fusion.5
  320.1 1.1 dynamic-slice_bitcast_fusion.5
  325.0 1.1 dynamic-slice_bitcast_fusion.5
  329.9 1.1 dynamic-slice_bitcast_fusion.5
  334.8 1.1 dynamic-slice_bitcast_fusion.5
  339.7 1.1 dynamic-slice_bitcast_fusion.5
  344.6 4.3 fusion.155
  348.9 65.2 %all-reduce.9.cloned.1.call-done = f32[128,4096]{1,0:T(8,128)} async-done(((f32[128,4096]{1,0:T(8,128)}), f32[128,4096]{1,0:T(8,128)}) %all-reduce.9.cloned.1.call-update) | async-done | bytes 2097168 | tf_op jit(solution)/shard_map/psum | solution.py:147
  414.2 2.0 fusion.88
  416.2 4.4 fusion.109
  420.6 9.0 %fusion.95 = f32[128,4096]{1,0:T(8,128)} fusion(bf16[896,4096]{1,0:T(8,128)(2,1)} %param.33, bf16[4096,896]{1,0:T(8,128)(2,1)} %all-gather.5.cloned.1.call-done, f32[128,896]{1,0:T(8,128)S(1)} %fusion.109, bf16[128,4096]{1,0:T(8,128)(2,1)S(1)} %get-tuple-element.156, f32[128]{0:T(128)S(1)} %add_rsqrt_fusion, f32[4096]{0:T(1024)S(1)} %copy-done.6), kind=kOutput, calls=%fused_computation.147 | convolution fusion | flops 1881833472 | bytes 18301440 | tf_op jit(solution)/shard_map/dot_general | solution.py:157
  429.6 65.3 %all-reduce.11.cloned.1.call-done = f32[128,4096]{1,0:T(8,128)} async-done(((f32[128,4096]{1,0:T(8,128)}), f32[128,4096]{1,0:T(8,128)}) %all-reduce.11.cloned.1.call-update) | async-done | bytes 2097168 | tf_op jit(solution)/shard_map/psum | solution.py:157
  494.9 2.8 fusion.91
  (328 shorter events, 57.0 us)
Async XLA Ops:
  7.4 1.9 copy-start
  7.4 145.3 %all-reduce.5.cloned.1.call-start = ((), (), s32[]{:S(2)}) async-start(), calls=%async_computation | async-start | bytes 4194304 | tf_op jit(solution)/shard_map/psum | solution.py:147
  7.4 9.0 %copy-start.9 = (f32[64]{0:T(128)}, f32[64]{0:T(128)S(1)}, u32[]{:S(2)}) copy-start(f32[64]{0:T(128)S(1)} %multiply_power_fusion) | copy-start | bytes 772
  9.3 3.3 copy-start.14
  9.3 3.5 copy-start.2
  9.3 3.5 copy-start.11
  12.8 3.6 copy-start.7
  25.2 6.5 %copy-start.5 = (bf16[1,512,256]{2,1,0:T(8,128)(2,1)S(1)}, bf16[1,512,256]{2,1,0:T(8,128)(2,1)}, u32[]{:S(2)}) copy-start(bf16[1,512,256]{2,1,0:T(8,128)(2,1)} %param.24) | copy-start | bytes 786436
  83.0 72.5 %all-gather.3.cloned.1.call-start = ((), (), s32[]{:S(2)}) async-start(), calls=%async_computation.1 | async-start | bytes 7798784 | tf_op jit(solution)/shard_map/all_gather | solution.py:151
  83.6 138.9 %all-gather.5.cloned.1.call-start = ((), (), s32[]{:S(2)}) async-start(), calls=%async_computation.2 | async-start | bytes 7798784 | tf_op jit(solution)/shard_map/all_gather | solution.py:152
  84.2 71.3 %copy-start.6 = (f32[4096]{0:T(1024)S(1)}, f32[4096]{0:T(1024)}, u32[]{:S(2)}) copy-start(f32[4096]{0:T(1024)} %param.30) | copy-start | bytes 49156
  84.2 212.6 %all-reduce.7.cloned.1.call-start = ((), (), s32[]{:S(2)}) async-start(), calls=%async_computation.3 | async-start | bytes 4194304 | tf_op jit(solution)/shard_map/psum | solution.py:157
  231.5 182.6 %all-reduce.9.cloned.1.call-start = ((), (), s32[]{:S(2)}) async-start(), calls=%async_computation.4 | async-start | bytes 4194304 | tf_op jit(solution)/shard_map/psum | solution.py:147
  296.9 3.5 copy-start.12
  299.4 1.0 copy-start.3
  300.3 0.7 copy-start.13
  301.1 3.3 copy-start.8
  301.1 3.3 copy-start.10
  304.4 1.0 copy-start.15
  348.8 65.3 %copy-start.4 = (bf16[128,4096]{1,0:T(8,128)(2,1)S(1)}, bf16[128,4096]{1,0:T(8,128)(2,1)}, u32[]{:S(2)}) copy-start(bf16[128,4096]{1,0:T(8,128)(2,1)} %copy-done.3) | copy-start | bytes 3145732
  348.9 146.0 %all-reduce.11.cloned.1.call-start = ((), (), s32[]{:S(2)}) async-start(), calls=%async_computation.5 | async-start | bytes 4194304 | tf_op jit(solution)/shard_map/psum | solution.py:157
  429.6 68.0 %copy-start.1 = (bf16[4096,256]{1,0:T(8,128)(2,1)S(1)}, bf16[4096,256]{1,0:T(8,128)(2,1)}, u32[]{:S(2)}) copy-start(bf16[4096,256]{1,0:T(8,128)(2,1)} %param.28) | copy-start | bytes 6291460
Sparse Core Ops, SparseCore 0:
  83.2 69.5 all-reduce.4
  231.7 65.1 all-reduce.6
  349.0 65.1 all-reduce.8
  429.7 65.1 all-reduce.10
Sparse Core Ops, SparseCore 1:
  85.7 68.7 all-gather.2
  156.6 65.9 all-gather.4
where the time goes:
time: 507 us; the launch traced here: 505 us
  waiting for transfers between devices  326 us (64%)
  matrix products  72.5 us (14%)
  local copies, waits for them, and re-layouts  45.8 us (9%)
  other arithmetic  43.5 us (9%)
  between operations  15.6 us (3%)
    psum x2, waiting for transfers between devices, one_pass(): lax.psum(jnp.dot(attended, w_o, preferred_element_type=jnp.float32), 'mlp')  134 us
    psum x2, waiting for transfers between devices, one_pass(): lax.psum(jnp.dot(hidden, w_down, preferred_element_type=jnp.float32), 'mlp')  129 us
    all_gather x1, waiting for transfers between devices, one_pass(): lax.all_gather(w_up, 'req', axis=0, tiled=True)  61.8 us
    dot_general x2, matrix products, one_pass(): jnp.dot(hidden, w_down, preferred_element_type=jnp.float32)  18 us
    squeeze x16, local copies, waits for them, and re-layouts, one_pass(): lax.map(attend_request, (queries.reshape(REQS, BLOCK, local_heads, HEAD_D...  17.3 us
    dot_general x48, matrix products, scores(): jnp.einsum('tkgd,lkd->kgtl', grouped, keys, preferred_element_type=jnp.fl...  11.7 us
    lt x16, other arithmetic, attend_one(): prompt_ok = jnp.arange(prompt_part.shape[0], dtype=jnp.int32) < prompt_size  10.5 us
    lt x16, other arithmetic, attend_one(): cache_ok = jnp.arange(cached_part.shape[0], dtype=jnp.int32) < cache_size  10.4 us
  transfers between devices with their start and end apart: 6, of which 5 were waited for; matrix products, arithmetic and copies ran while one was open for 2% of the time, Pallas kernels for 0%

commit v1 on v0

--- a/solution.py
+++ b/solution.py
@@ -149,7 +149,9 @@
         normed2 = rms_scale(after_attn, mlp_gain)
         pass_gate, pass_up = (
             lax.all_gather(w_gate, "req", axis=0, tiled=True),
-            lax.all_gather(w_up, "req", axis=0, tiled=True),
+            jnp.concatenate(
+                lax.all_to_all(jnp.stack([w_up] * lax.axis_size("req")), "req", 0, 0), axis=0
+            ),
         )
         gate = jnp.dot(normed2, pass_gate, preferred_element_type=jnp.float32)
         up_part = jnp.dot(normed2, pass_up, preferred_element_type=jnp.float32)

time: 507 us -> 551 us (1.087)
  waiting for transfers between devices: 326 us -> 348 us
  local copies, waits for them, and re-layouts: 45.8 us -> 55.8 us
  starting transfers between devices: 0.39 us -> 8.51 us
    all_gather x1, waiting for transfers between devices: 0.01 us -> 92.3 us  [one_pass(): lax.all_gather(w_gate, 'req', axis=0, tiled=True)]
    all_gather x1 -> x0, waiting for transfers between devices: 61.8 us -> none  [one_pass(): lax.all_gather(w_up, 'req', axis=0, tiled=True)]
    psum x2, waiting for transfers between devices: 134 us -> 122 us  [one_pass(): lax.psum(jnp.dot(attended, w_o, preferred_element_type=jnp.float32), 'mlp')]
    all_to_all x0 -> x1, starting transfers between devices: none -> 8.16 us  [one_pass(): lax.all_to_all(jnp.stack([w_up] * lax.axis_size('req')), 'req', 0, 0)]
    dot_general x16, matrix products: 8.76 us -> 14.3 us  [attend_one(): jnp.einsum('kgtl,lkd->tkgd', block_w, block_values, preferred_element_typ...]
where the time goes in v1:
time: 551 us; the launch traced here: 549 us
  waiting for transfers between devices  348 us (63%)
  matrix products  77.5 us (14%)
  local copies, waits for them, and re-layouts  55.8 us (10%)
  other arithmetic  42.7 us (8%)
  between operations  15.6 us (3%)
  starting transfers between devices  8.51 us (2%)
    psum x2, waiting for transfers between devices, one_pass(): lax.psum(jnp.dot(hidden, w_down, preferred_element_type=jnp.float32), 'mlp')  133 us
    psum x2, waiting for transfers between devices, one_pass(): lax.psum(jnp.dot(attended, w_o, preferred_element_type=jnp.float32), 'mlp')  122 us
    all_gather x1, waiting for transfers between devices, one_pass(): lax.all_gather(w_gate, 'req', axis=0, tiled=True)  92.3 us
    dot_general x2, matrix products, one_pass(): jnp.dot(hidden, w_down, preferred_element_type=jnp.float32)  18.3 us
    squeeze x16, local copies, waits for them, and re-layouts, one_pass(): lax.map(attend_request, (queries.reshape(REQS, BLOCK, local_heads, HEAD_D...  17.3 us
    dynamic_slice x16, local copies, waits for them, and re-layouts, one_pass(): lax.map(attend_request, (queries.reshape(REQS, BLOCK, local_heads, HEAD_D...  15.7 us
    dot_general x16, matrix products, attend_one(): jnp.einsum('kgtl,lkd->tkgd', block_w, block_values, preferred_element_typ...  14.3 us
    dot_general x48, matrix products, scores(): jnp.einsum('tkgd,lkd->kgtl', grouped, keys, preferred_element_type=jnp.fl...  11.7 us
  transfers between devices with their start and end apart: 6, of which 5 were waited for; matrix products, arithmetic and copies ran while one was open for 2% of the time, Pallas kernels for 0%

profile of v1, /device:TPU:0, one launch (start us, length us, event | category | flops | bytes accessed | tf_op | source)
XLA Modules:
  0.0 548.7 jit_solution(9528408026434702988)
XLA Ops:
  7.4 1.7 fusion.76
  9.3 1.8 fusion.119
  11.9 3.7 fusion.121
  15.6 1.0 reshape.550
  18.0 6.5 %copy.26 = bf16[1,8,1024,256]{2,3,1,0:T(8,128)(2,1)} copy(bf16[1,8,1024,256]{3,2,1,0:T(8,128)(2,1)} %param.25) | data formatting | bytes 8388608 | tf_op args[6]
  24.4 6.5 %copy.30 = bf16[8,1024,1,2,128]{4,1,3,2,0:T(8,128)(2,1)} copy(bf16[8,1024,1,2,128]{1,4,3,0,2:T(8,128)(2,1)} %bitcast.295) | data formatting | bytes 8388608 | tf_op jit(solution)/shard_map/while | solution.py:136
  32.6 45.0 %while.20 = (s32[]{:T(128)}, bf16[8,16,512]{2,1,0:T(8,128)(2,1)S(1)}, s32[]{:T(128)}, bf16[8,16,4,128]{3,1,0,2:T(8,128)(2,1)S(1)}, bf16[512,1,2,128]{3,0,2,1:T(8...) while((s32[]{:T(128)}, ...), condition=%wide.region_8.9_spmd, body=%wide.region_1.8_spmd.sunk | while | flops 51675520 | bytes 3347349 | solution.py:136
  32.6 1.1 dynamic-slice_bitcast_fusion.4
  37.3 0.9 fusion.211
  38.2 1.1 dynamic-slice_bitcast_fusion.4
  42.9 0.9 fusion.211
  43.8 1.1 dynamic-slice_bitcast_fusion.4
  48.5 0.9 fusion.211
  49.5 1.1 dynamic-slice_bitcast_fusion.4
  54.1 0.9 fusion.211
  55.1 1.1 dynamic-slice_bitcast_fusion.4
  59.8 0.9 fusion.211
  60.7 1.1 dynamic-slice_bitcast_fusion.4
  65.4 0.9 fusion.211
  66.3 1.1 dynamic-slice_bitcast_fusion.4
  71.0 0.9 fusion.211
  72.0 1.1 dynamic-slice_bitcast_fusion.4
  76.6 0.9 fusion.211
  77.6 4.3 fusion.154
  82.9 4.0 stack.2
  86.9 8.2 %all-to-all-start = ((bf16[16,256,896]{2,1,0:T(8,128)(2,1)}), bf16[16,256,896]{2,1,0:T(8,128)(2,1)}, u32[]{:S(2)}, u32[]{:S(2)}) async-start(bf16[16,256,896]{2,1,0:T(8,128)(2,1)} %stack.2), calls=%async_computation | async-start | bytes 14680064 | tf_op jit(solution)/shard_map/all_to_all | solution.py:153
  95.1 56.7 %all-reduce.5.cloned.1.call-done = f32[128,4096]{1,0:T(8,128)} async-done(((f32[128,4096]{1,0:T(8,128)}), f32[128,4096]{1,0:T(8,128)}) %all-reduce.5.cloned.1.call-update) | async-done | bytes 2097168 | tf_op jit(solution)/shard_map/psum | solution.py:147
  151.8 2.3 fusion.80
  154.7 92.3 %all-gather.2.cloned.1.call-done = bf16[4096,896]{1,0:T(8,128)(2,1)} async-done(((bf16[256,896]{1,0:T(8,128)(2,1)}), bf16[4096,896]{1,0:T(8,128)(2,1)}) %all-gather.2.cloned.1.call-update) | async-done | bytes 7340048 | tf_op jit(solution)/shard_map/all_gather | solution.py:151
  247.0 5.2 fusion.117
  252.2 9.1 %fusion.96 = f32[128,4096]{1,0:T(8,128)} fusion(bf16[896,4096]{1,0:T(8,128)(2,1)} %param.33, bf16[4096,896]{1,0:T(8,128)(2,1)} %bitcast.70, f32[128,896]{1,0:T(8,128)} %fusion.117, bf16[128,4096]{1,0:T(8,128)(2,1)S(1)} %get-tuple-element.160, f32[4096]{0:T(1024)S(1)} %copy-done.7, f32[128]{0:T(128)} %add_rsqrt_fusion.2), kind=kOutput, calls=%fused_computation.148 | convolution fusion | flops 1881833472 | bytes 18301440 | tf_op jit(solution)/shard_map/dot_general | solution.py:159
  261.5 1.2 broadcast_compare_fusion
  262.7 67.5 %all-reduce.7.cloned.1.call-done = f32[128,4096]{1,0:T(8,128)} async-done(((f32[128,4096]{1,0:T(8,128)}), f32[128,4096]{1,0:T(8,128)}) %all-reduce.7.cloned.1.call-update) | async-done | bytes 2097168 | tf_op jit(solution)/shard_map/psum | solution.py:159
  330.2 2.7 fusion.84
  336.5 50.9 %while.21 = (s32[]{:T(128)}, bf16[8,16,512]{2,1,0:T(8,128)(2,1)S(1)}, s32[]{:T(128)}, bf16[8,16,4,128]{3,1,0,2:T(8,128)(2,1)S(1)}, bf16[512,1,2,128]{3,0,2,1:T(8...) while((s32[]{:T(128)}, ...), condition=%wide.region_20.21_spmd, body=%wide.region_13.20_spmd.sunk | while | flops 51675520 | bytes 3347349 | solution.py:136
  336.5 1.1 dynamic-slice_bitcast_fusion.5
  337.6 1.3 dynamic_slice.119
  341.9 0.9 fusion.225
  342.8 1.1 dynamic-slice_bitcast_fusion.5
  343.9 1.3 dynamic_slice.119
  348.2 0.9 fusion.225
  349.2 1.1 dynamic-slice_bitcast_fusion.5
  350.3 1.3 dynamic_slice.119
  354.6 0.9 fusion.225
  355.6 1.1 dynamic-slice_bitcast_fusion.5
  356.6 1.3 dynamic_slice.119
  361.0 0.9 fusion.225
  361.9 1.1 dynamic-slice_bitcast_fusion.5
  363.0 1.3 dynamic_slice.119
  367.3 0.9 fusion.225
  368.3 1.1 dynamic-slice_bitcast_fusion.5
  369.4 1.3 dynamic_slice.119
  373.7 0.9 fusion.225
  374.6 1.1 dynamic-slice_bitcast_fusion.5
  375.7 1.3 dynamic_slice.119
  381.0 1.1 dynamic-slice_bitcast_fusion.5
  382.1 1.3 dynamic_slice.119
  387.4 4.3 fusion.155
  391.7 65.2 %all-reduce.9.cloned.1.call-done = f32[128,4096]{1,0:T(8,128)} async-done(((f32[128,4096]{1,0:T(8,128)}), f32[128,4096]{1,0:T(8,128)}) %all-reduce.9.cloned.1.call-update) | async-done | bytes 2097168 | tf_op jit(solution)/shard_map/psum | solution.py:147
  456.9 2.3 fusion.88
  459.2 5.2 fusion.109
  464.4 9.2 %fusion.95 = f32[128,4096]{1,0:T(8,128)} fusion(bf16[896,4096]{1,0:T(8,128)(2,1)} %param.33, bf16[4096,896]{1,0:T(8,128)(2,1)} %bitcast.70, f32[128,896]{1,0:T(8,128)} %fusion.109, bf16[128,4096]{1,0:T(8,128)(2,1)S(1)} %get-tuple-element.156, f32[128]{0:T(128)S(1)} %add_rsqrt_fusion, f32[4096]{0:T(1024)S(1)} %copy-done.7), kind=kOutput, calls=%fused_computation.147 | convolution fusion | flops 1881833472 | bytes 18301440 | tf_op jit(solution)/shard_map/dot_general | solution.py:159
  473.5 65.3 %all-reduce.11.cloned.1.call-done = f32[128,4096]{1,0:T(8,128)} async-done(((f32[128,4096]{1,0:T(8,128)}), f32[128,4096]{1,0:T(8,128)}) %all-reduce.11.cloned.1.call-update) | async-done | bytes 2097168 | tf_op jit(solution)/shard_map/psum | solution.py:159
  538.8 2.8 fusion.91
  (327 shorter events, 63.0 us)
Async XLA Ops:
  7.4 1.9 copy-start
  7.4 144.4 %all-reduce.5.cloned.1.call-start = ((), (), s32[]{:S(2)}) async-start(), calls=%async_computation.1 | async-start | bytes 4194304 | tf_op jit(solution)/shard_map/psum | solution.py:147
  7.4 23.9 %copy-start.10 = (f32[64]{0:T(128)}, f32[64]{0:T(128)S(1)}, u32[]{:S(2)}) copy-start(f32[64]{0:T(128)S(1)} %multiply_power_fusion) | copy-start | bytes 772
  9.3 2.6 copy-start.1
  11.2 4.4 copy-start.3
  11.9 5.6 %copy-start.14 = (s32[1,8]{1,0:T(1,128)S(1)}, s32[1,8]{1,0:T(1,128)}, u32[]{:S(2)}) copy-start(s32[1,8]{1,0:T(1,128)} %param.23) | copy-start | bytes 100
  11.9 5.8 %copy-start.5 = (bf16[1,512,256]{2,1,0:T(8,128)(2,1)S(1)}, bf16[1,512,256]{2,1,0:T(8,128)(2,1)}, u32[]{:S(2)}) copy-start(bf16[1,512,256]{2,1,0:T(8,128)(2,1)} %param.24) | copy-start | bytes 786436
  17.7 13.6 %copy-start.8 = (f32[128]{0:T(128)}, f32[128]{0:T(128)S(1)}, u32[]{:S(2)}) copy-start(f32[128]{0:T(128)S(1)} %convert_element_type.168) | copy-start | bytes 1540
  24.4 6.9 %slice-start = ((f32[128,1,2,128]{3,2,0,1:T(2,128)}), f32[128,1,1,128]{3,2,0,1:T(1,128)S(1)}, s32[]{:S(2)}) async-start(f32[128,1,2,128]{3,2,0,1:T(2,128)} %copy-done.3), calls=%async_computation.6 | async-start | bytes 131072 | tf_op jit(solution)/shard_map/slice | solution.py:127
  24.4 7.2 %copy-start.6 = (bf16[128,1,1,128]{3,2,0,1:T(2,128)(2,1)S(1)}, bf16[128,1,1,128]{3,2,0,1:T(2,128)(2,1)}, u32[]{:S(2)}) copy-start(bf16[128,1,1,128]{3,2,0,1:T(2,128)(2,1)} %slice.83) | copy-start | bytes 98308
  81.9 1.0 copy-start.4
  81.9 165.0 %all-gather.2.cloned.1.call-start = ((), (), s32[]{:S(2)}) async-start(), calls=%async_computation.2 | async-start | bytes 7798784 | tf_op jit(solution)/shard_map/all_gather | solution.py:151
  86.9 165.3 %all-to-all-start = ((bf16[16,256,896]{2,1,0:T(8,128)(2,1)}), bf16[16,256,896]{2,1,0:T(8,128)(2,1)}, u32[]{:S(2)}, u32[]{:S(2)}) async-start(bf16[16,256,896]{2,1,0:T(8,128)(2,1)} %stack.2), calls=%async_computation | async-start | bytes 14680064 | tf_op jit(solution)/shard_map/all_to_all | solution.py:153
  95.1 151.9 %copy-start.7 = (f32[4096]{0:T(1024)S(1)}, f32[4096]{0:T(1024)}, u32[]{:S(2)}) copy-start(f32[4096]{0:T(1024)} %param.30) | copy-start | bytes 49156
  95.1 235.1 %all-reduce.7.cloned.1.call-start = ((), (), s32[]{:S(2)}) async-start(), calls=%async_computation.3 | async-start | bytes 4194304 | tf_op jit(solution)/shard_map/psum | solution.py:159
  261.3 195.6 %all-reduce.9.cloned.1.call-start = ((), (), s32[]{:S(2)}) async-start(), calls=%async_computation.4 | async-start | bytes 4194304 | tf_op jit(solution)/shard_map/psum | solution.py:147
  330.2 3.1 copy-start.12
  330.2 3.1 copy-start.13
  332.8 1.3 copy-start.2
  334.2 1.1 copy-start.9
  334.2 1.1 copy-start.11
  391.6 147.2 %all-reduce.11.cloned.1.call-start = ((), (), s32[]{:S(2)}) async-start(), calls=%async_computation.5 | async-start | bytes 4194304 | tf_op jit(solution)/shard_map/psum | solution.py:159
Sparse Core Ops, SparseCore 0:
  82.1 69.6 all-reduce.4
  261.4 68.7 all-reduce.6
  391.8 65.1 all-reduce.8
  473.7 65.1 all-reduce.10
Sparse Core Ops, SparseCore 1:
  84.6 162.3 all-gather.1
